TPU v7x, 256 devices: a whole 4x4x8 slice. The times are simulated.
256 devices in a mesh: group: 4 (over x), owner: 64 (over z, y, core).
Axes of the slice: x: 4, y: 4, z: 8, core: 2. Of those that a mesh axis runs over, the one named last changes fastest.
Arguments:
- embeddings: bfloat16 [393216, 1024], P(('group', 'owner')), may hold values from -40 to 40
- assignment: int32 [393216, 1], P(('group', 'owner')), may hold values from 0 to 255, as said below
- home_map: int32 [256], replicated, may hold values from 0 to 255, each once
Outputs:
- centroids: float32 [256, 1024], P('owner')
- nearest: float32 [393216], P(('group', 'owner'))
- centrality: float32 [393216], P(('group', 'owner'))
Inputs may be any that keep to these rules, and one draw needn't show every extreme that they name: `assignment`: in the rows of one device no cluster id occurs more than 12 times; the same quarter of the clusters occurs exactly 12 times in every device's rows. `home_map`: each home slot once.
All inputs are finite; a program needn't handle non-finite values.
Results may differ from a plain program's by a relative error of at most 0.00048.
Values may be sent and summed in bfloat16 or wider, within the bound.
A program may use at most 64 MiB of HBM per device.

v0:
```python
import jax
import jax.numpy as jnp
from jax import lax
from jax.sharding import PartitionSpec as P

CAP = 12


def normalize_rows(descriptor_vectors):
    values = descriptor_vectors.astype(jnp.float32)
    return values * lax.rsqrt(jnp.mean(values * values, axis=-1, keepdims=True) + 1e-06)


def body(embeddings, assignment, home_map):
    owners = lax.axis_size("owner")
    clusters = home_map.shape[0]
    per_owner = clusters // owners
    feature_count = embeddings.shape[1]
    cluster_ids = assignment[:, 0]
    table_index = jnp.arange(clusters, dtype=jnp.int32)
    matches = cluster_ids[:, None] == table_index[None, :]
    home_slot = jnp.sum(jnp.where(matches, home_map[None, :], 0), axis=1)
    running = jnp.cumsum(matches.astype(jnp.int32), axis=0)
    rank_in_block = jnp.sum(jnp.where(matches, running, 0), axis=1) - 1
    targets = home_slot * CAP + rank_in_block
    normed = normalize_rows(embeddings).astype(jnp.bfloat16)
    outgoing = jnp.zeros((clusters * CAP, feature_count), jnp.bfloat16).at[targets].set(normed)
    slot_marks = jnp.zeros((clusters * CAP,), jnp.bfloat16).at[targets].set(1.0)
    members, present = (
        lax.all_to_all(
            outgoing.reshape(owners, per_owner, CAP, feature_count),
            "owner",
            split_axis=0,
            concat_axis=0,
            tiled=True,
        ),
        lax.all_to_all(
            slot_marks.reshape(owners, per_owner, CAP),
            "owner",
            split_axis=0,
            concat_axis=0,
            tiled=True,
        ),
    )
    wanted = jnp.arange(per_owner * lax.axis_size("owner"), dtype=jnp.int32)
    onehot = (wanted[:, None] == home_slot[None, :]).astype(jnp.bfloat16)
    own_sums = lax.psum_scatter(
        jnp.dot(onehot, normed, preferred_element_type=jnp.float32),
        "owner",
        scatter_dimension=0,
        tiled=True,
    )
    cluster_totals = lax.psum(own_sums, "group")
    centroids = normalize_rows(cluster_totals)
    centroid_low = centroids.astype(jnp.bfloat16)
    similarity = (
        jnp.einsum("acpd,bcqd->acpbq", members, members, preferred_element_type=jnp.float32)
        / feature_count
    )
    source_identity_matrix = jnp.eye(owners, dtype=jnp.bool_)
    slot_eye = jnp.eye(CAP, dtype=jnp.bool_)
    self_pair = source_identity_matrix[:, None, None, :, None] & slot_eye[None, None, :, None, :]
    key_marks = jnp.transpose(present, (1, 0, 2))[None, :, None, :, :] > 0
    allowed = key_marks & ~self_pair
    nearest = jnp.max(jnp.where(allowed, similarity, -1.0), axis=(3, 4))
    centrality = (
        jnp.einsum("acpd,cd->acp", members, centroid_low, preferred_element_type=jnp.float32)
        / feature_count
    )
    nearest_back, central_back = (
        lax.all_to_all(nearest, "owner", split_axis=0, concat_axis=0, tiled=True),
        lax.all_to_all(centrality, "owner", split_axis=0, concat_axis=0, tiled=True),
    )
    nearest_rows = jnp.take(nearest_back.reshape(-1), targets)
    central_rows = jnp.take(central_back.reshape(-1), targets)
    return (centroids, nearest_rows, central_rows)


def solution(mesh):
    in_specs = (P(("group", "owner"), None), P(("group", "owner"), None), P())
    out_specs = (P("owner", None), P(("group", "owner")), P(("group", "owner")))
    return jax.shard_map(body, mesh=mesh, in_specs=in_specs, out_specs=out_specs, check_vma=False)
```

profile of v0, /device:TPU:1, one launch (start us, length us, event | category | flops | bytes accessed | tf_op | source)
XLA Modules:
  0.0 435.0 jit_solution(8718678912319985145)
XLA Ops:
  7.2 0.7 reduce
  7.9 0.1 copy.17
  8.0 0.3 fusion.10
  8.4 0.0 copy-start.1
  8.4 0.2 broadcast_add_fusion
  8.6 0.0 copy-start
  8.6 0.9 copy.18
  9.6 0.0 copy-done.1
  9.6 0.8 fusion.12
  10.5 11.1 %scatter_custom_fusion = bf16[3072]{0:T(1024)(128)(2,1)S(1)} fusion(s32[1536]{0:T(1024)S(1)} %fusion.20, bf16[1536]{0:T(1024)(128)(2,1)S(1)} %broadcast.112, bf16[]{:T(256)} %constant.23.clone.1), kind=kCustom, calls=%fused_computation.49 | custom fusion | bytes 6146 | tf_op jit(solution)/shard_map/scatter | solution.py:28
  21.6 0.8 reshape.113
  22.3 13.5 %all-to-all-start = ((bf16[64,4,12]{2,1,0:T(4,128)(2,1)}), bf16[64,4,12]{2,1,0:T(4,128)(2,1)S(1)}, u32[]{:S(2)}, u32[]{:S(2)}) async-start(bf16[64,4,12]{2,1,0:T(4,128)(2,1)} %reshape.113), calls=%async_computation | async-start | bytes 131072 | tf_op jit(solution)/shard_map/all_to_all | solution.py:37
  35.9 0.0 copy-done
  35.9 0.7 fusion.1
  36.6 12.0 %scatter_custom_fusion.1 = bf16[3072,1024]{1,0:T(8,128)(2,1)} fusion(s32[1536]{0:T(1024)S(1)} %fusion.20, bf16[]{:T(256)} %constant.23.clone.1, bf16[1536,1024]{1,0:T(8,128)(2,1)S(1)} %copy-done, f32[1536]{0:T(1024)S(1)} %add_rsqrt_fusion), kind=kCustom, calls=%fused_computation.16 | custom fusion | flops 4718592 | bytes 9445378 | tf_op jit(solution)/shard_map/scatter | solution.py:27
  48.6 11.1 %reshape.114 = bf16[64,4,12,1024]{3,2,1,0:T(8,128)(2,1)} reshape(bf16[3072,1024]{1,0:T(8,128)(2,1)} %scatter_custom_fusion.1) | data formatting | bytes 12582912 | tf_op jit(solution)/shard_map/reshape | solution.py:31
  59.7 18.8 %copy.20 = bf16[64,4,12,1024]{3,1,2,0:T(4,128)(2,1)} copy(bf16[64,4,12,1024]{3,2,1,0:T(8,128)(2,1)} %reshape.114) | data formatting | bytes 12582912 | tf_op jit(solution)/shard_map/reshape | solution.py:31
  78.5 0.0 all-to-all-done
  78.5 10.5 %all-to-all-start.1 = ((bf16[64,4,12,1024]{3,1,2,0:T(4,128)(2,1)}), bf16[64,4,12,1024]{3,1,2,0:T(4,128)(2,1)}, u32[]{:S(2)}, u32[]{:S(2)}) async-start(bf16[64,4,12,1024]{3,1,2,0:T(4,128)(2,1)} %copy.20), calls=%async_computation.1 | async-start | bytes 12582912 | tf_op jit(solution)/shard_map/all_to_all | solution.py:30
  89.0 0.0 copy-start.2
  89.0 0.0 all-reduce.3.cloned.1.call-start
  89.0 2.1 fusion.13
  91.2 0.0 all-reduce.3.cloned.1.call-update
  91.2 0.0 copy-done.2
  91.2 0.6 dynamic-slice
  92.5 0.7 and_not_fusion
  93.2 0.1 copy.19
  93.4 218.6 %all-reduce.3.cloned.1.call-done = f32[256,1024]{1,0:T(8,128)} async-done(((f32[256,1024]{1,0:T(8,128)}), f32[256,1024]{1,0:T(8,128)}) %all-reduce.3.cloned.1.call-update) | async-done | bytes 1048592
  311.9 0.8 constant_dynamic-slice_fusion
  312.7 13.1 %psum.7 = f32[4,1024]{1,0:T(4,128)S(1)} all-reduce(f32[4,1024]{1,0:T(4,128)S(1)} %constant_dynamic-slice_fusion), channel_id=1, replica_groups=mesh['group'=4,'owner'=64] {'group'}, use_global_device_ids=true, to_apply=%region_3.4 | all-reduce | flops 4096 | bytes 32768 | tf_op jit(solution)/shard_map/psum | solution.py:53
  325.8 0.1 multiply_reduce_fusion
  325.9 0.7 convert_bitcast_fusion
  326.6 0.0 all-to-all-done.1
  326.6 46.5 %fusion = f32[64,4,12]{0,2,1:T(8,128)S(1)} fusion(pred[64,12,64,12]{0,2,1,3:T(8,128)(4,1)S(1)} %and_not_fusion, pred[4,64,12]{1,2,0:T(8,128)(4,1)S(1)} %copy.19, bf16[64,4,12,1024,1]{3,1,2,0,4:T(4,128)(2,1)} %bitcast.4, bf16[64,4,12,1024]{3,1,2,0:T(4,128)(2,1)} %all-to-all-done.1), kind=kOutput, calls=%fused_computation.5 | convolution fusion | flops 4841272320 | bytes 13188096 | tf_op jit(solution)/shard_map/acpd,bcqd->acpbq/dot_general | solution.py:57
  373.1 0.8 copy.23
  373.8 12.7 %all-to-all-start.2 = ((f32[64,4,12]{2,1,0:T(4,128)}), f32[64,4,12]{2,1,0:T(4,128)S(1)}, u32[]{:S(2)}, u32[]{:S(2)}) async-start(f32[64,4,12]{2,1,0:T(4,128)} %copy.23), calls=%async_computation.2 | async-start | bytes 262144 | tf_op jit(solution)/shard_map/all_to_all | solution.py:71
  386.6 9.4 %fusion.5 = f32[4,1,64,12]{2,1,3,0:T(1,128)S(1)} fusion(bf16[64,4,12,1024]{3,1,2,0:T(4,128)(2,1)} %all-to-all-done.1, bf16[4,1024,1,1]{1,0,2,3:T(4,128)(2,1)S(1)} %get-tuple-element.8), kind=kOutput, calls=%fused_computation.12 | convolution fusion | flops 6291456 | bytes 6311936 | tf_op jit(solution)/shard_map/acpd,cd->acp/dot_general | solution.py:67
  396.0 0.1 copy.27
  396.1 0.7 fusion.18
  396.8 0.8 all-to-all-done.2
  397.5 9.5 %all-to-all-start.3 = ((f32[64,4,12]{2,1,0:T(4,128)}), f32[64,4,12]{2,1,0:T(4,128)S(1)}, u32[]{:S(2)}, u32[]{:S(2)}) async-start(f32[64,4,12]{2,1,0:T(4,128)} %fusion.18), calls=%async_computation.3 | async-start | bytes 262144 | tf_op jit(solution)/shard_map/all_to_all | solution.py:72
  407.1 0.2 reshape.115
  407.3 8.4 %gather_fusion = f32[1536]{0:T(1024)S(1)} fusion(f32[3072]{0:T(1024)S(1)} %reshape.115, s32[2048]{0:T(1024)S(1)} %pad_clamp_fusion), kind=kCustom, calls=%fused_computation.clone | custom fusion | bytes 18432 | tf_op jit(solution)/shard_map/jit(_take)/gather | solution.py:74
  415.6 2.5 all-to-all-done.3
  418.2 0.2 reshape.116
  418.3 8.4 %gather_fusion.1 = f32[1536]{0:T(1024)S(1)} fusion(f32[3072]{0:T(1024)S(1)} %reshape.116, s32[2048]{0:T(1024)S(1)} %pad_clamp_fusion), kind=kCustom, calls=%fused_computation.1.clone | custom fusion | bytes 18432 | tf_op jit(solution)/shard_map/jit(_take)/gather | solution.py:75
  426.7 0.6 broadcast_select_fusion
  427.3 0.6 broadcast_select_fusion.1
  (11 shorter events, 0.2 us)
Async XLA Ops:
  8.4 1.2 copy-start.1
  8.6 27.3 %copy-start = (bf16[1536,1024]{1,0:T(8,128)(2,1)S(1)}, bf16[1536,1024]{1,0:T(8,128)(2,1)}, u32[]{:S(2)}) copy-start(bf16[1536,1024]{1,0:T(8,128)(2,1)} %param.5) | copy-start | bytes 9437188
  22.3 56.2 %all-to-all-start = ((bf16[64,4,12]{2,1,0:T(4,128)(2,1)}), bf16[64,4,12]{2,1,0:T(4,128)(2,1)S(1)}, u32[]{:S(2)}, u32[]{:S(2)}) async-start(bf16[64,4,12]{2,1,0:T(4,128)(2,1)} %reshape.113), calls=%async_computation | async-start | bytes 131072 | tf_op jit(solution)/shard_map/all_to_all | solution.py:37
  78.5 248.1 %all-to-all-start.1 = ((bf16[64,4,12,1024]{3,1,2,0:T(4,128)(2,1)}), bf16[64,4,12,1024]{3,1,2,0:T(4,128)(2,1)}, u32[]{:S(2)}, u32[]{:S(2)}) async-start(bf16[64,4,12,1024]{3,1,2,0:T(4,128)(2,1)} %copy.20), calls=%async_computation.1 | async-start | bytes 12582912 | tf_op jit(solution)/shard_map/all_to_all | solution.py:30
  89.0 2.2 copy-start.2
  89.0 222.9 %all-reduce.3.cloned.1.call-start = ((), (), s32[]{:S(2)}) async-start(), calls=%async_computation.4 | async-start | bytes 2097152
  373.8 23.7 %all-to-all-start.2 = ((f32[64,4,12]{2,1,0:T(4,128)}), f32[64,4,12]{2,1,0:T(4,128)S(1)}, u32[]{:S(2)}, u32[]{:S(2)}) async-start(f32[64,4,12]{2,1,0:T(4,128)} %copy.23), calls=%async_computation.2 | async-start | bytes 262144 | tf_op jit(solution)/shard_map/all_to_all | solution.py:71
  397.5 20.6 %all-to-all-start.3 = ((f32[64,4,12]{2,1,0:T(4,128)}), f32[64,4,12]{2,1,0:T(4,128)S(1)}, u32[]{:S(2)}, u32[]{:S(2)}) async-start(f32[64,4,12]{2,1,0:T(4,128)} %fusion.18), calls=%async_computation.3 | async-start | bytes 262144 | tf_op jit(solution)/shard_map/all_to_all | solution.py:72
Sparse Core Ops, SparseCore 0:
  93.2 218.6 all-reduce.2
where the time goes:
time: 441 us; the launch traced here: 435 us
  waiting for transfers between devices  222 us (50%)
  local copies, waits for them, and re-layouts  62.3 us (14%)
  matrix products  58 us (13%)
  starting transfers between devices  46.3 us (10%)
  other arithmetic  18.3 us (4%)
  between operations  15.1 us (3%)
  blocking collectives  13.1 us (3%)
    unnamed x2, waiting for transfers between devices  219 us
    dot_general x1, matrix products, body(): jnp.einsum('acpd,bcqd->acpbq', members, members, preferred_element_type=j...  46.5 us
    reshape x2, local copies, waits for them, and re-layouts, body(): outgoing.reshape(owners, per_owner, CAP, feature_count)  29.9 us
    all_to_all x1, starting transfers between devices, body(): lax.all_to_all(slot_marks.reshape(owners, per_owner, CAP), 'owner', split...  13.5 us
    psum x1, blocking collectives, body(): cluster_totals = lax.psum(own_sums, 'group')  13.1 us
    all_to_all x1, starting transfers between devices, body(): lax.all_to_all(nearest, 'owner', split_axis=0, concat_axis=0, tiled=True)  12.7 us
    scatter x1, other arithmetic, body(): jnp.zeros((clusters * CAP, feature_count), jnp.bfloat16).at[targets]  12 us
    scatter x1, local copies, waits for them, and re-layouts, body(): slot_marks = jnp.zeros((clusters * CAP,), jnp.bfloat16).at[targets].set(1.0)  11.1 us
  transfers between devices with their start and end apart: 5, of which 3 were waited for; matrix products, arithmetic and copies ran while one was open for 15% of the time, Pallas kernels for 0%

commit v1 on v0

v1 whole, which is shorter than its diff:
```python
import functools

import jax
import jax.numpy as jnp
from jax import lax
from jax.experimental import pallas as pl
from jax.experimental.pallas import tpu as pltpu
from jax.sharding import PartitionSpec as P

MESH = pl.DeviceIdType.MESH
F32 = jnp.float32
BF16 = jnp.bfloat16
I32 = jnp.int32

NZ, NY, NC = 8, 4, 2
NW = NY * NC
NX = 4
PLANE = 32
RANKS = 16
MARK = 128.0
NEG = -1e30
EPS = 1e-06


def dot(a, b):
    return lax.dot_general(a, b, (((1,), (0,)), ((), ())), preferred_element_type=F32)


def dot_t(a, b):
    return lax.dot_general(a, b, (((1,), (1,)), ((), ())), preferred_element_type=F32)


def iota(shape, axis):
    return lax.broadcasted_iota(I32, shape, axis)


def hot(mask):
    return jnp.where(mask, 1.0, 0.0).astype(BF16)


def z_order(i):
    return jnp.where(lax.rem(i, 2) == 0, 1 + i // 2, NZ - 1 - i // 2)


def kernel(cap, emb, ids, hm, cent_o, near_o, central_o, flag_o,
           normed, buf, meta, stage, mem, info, val, acc, flags, xbuf, near, ret, rz, rp, on_s, oc_s,
           zss, zrs, mss, mrs, iss, irs, xss, xrs, rss, rrs, pss, prs):
    rows, feat = emb.shape
    clusters = hm.shape[1]
    gx = lax.axis_index("group")
    me = lax.axis_index("owner")
    z, y, c = me // NW, lax.rem(me // NC, NY), lax.rem(me, NC)

    def z_dev(d):
        return lax.rem(z + d + NZ, NZ) * NW + y * NC + c

    def w_dev(e, sign):
        dy, dc = e // NC, lax.rem(e, NC)
        return z * NW + lax.rem(y + sign * dy + NY, NY) * NC + lax.rem(c + dc, NC)

    barrier = pltpu.get_barrier_semaphore()
    for d in range(1, NZ):
        pl.semaphore_signal(barrier, inc=1, device_id={"owner": z_dev(d)}, device_id_type=MESH)
    for e in range(1, NW):
        pl.semaphore_signal(barrier, inc=1, device_id={"owner": w_dev(e, 1)}, device_id_type=MESH)
    for k in range(1, NX):
        pl.semaphore_signal(barrier, inc=1, device_id={"group": lax.rem(gx + k, NX)}, device_id_type=MESH)

    h = hm[...]
    rel = (((h // PLANE - z + NZ) % NZ) * PLANE + ((h // 8 % NY - y + NY) % NY) * 8
           + ((h // 4 % NC + c) % NC) * 4 + h % 4)
    perm = hot(iota((clusters, clusters), 0) == rel)
    home = dot(perm, hot(iota((clusters, rows), 0) == ids[...])).astype(BF16)
    before = hot(iota((256, 256), 0) < iota((256, 256), 1))
    same = hot(iota((clusters, clusters), 0) // PLANE == iota((clusters, clusters), 1) // PLANE)
    base = jnp.zeros((clusters, 1), F32)
    number = iota((clusters, 256), 0).astype(F32)
    for k in range(rows // 256):
        part = home[:, k * 256:(k + 1) * 256]
        count = dot(part, before) + base
        wide = part.astype(F32)
        lanes = pl.ds(k * 256, 256)
        info[0:1, lanes] = jnp.sum(wide * number, axis=0, keepdims=True)
        info[1:2, lanes] = jnp.sum(wide * count, axis=0, keepdims=True)
        info[2:3, lanes] = jnp.sum(dot(same, part) * count, axis=0, keepdims=True)
        base = base + jnp.sum(wide, axis=1, keepdims=True)
    rel_home = info[0:1, :].astype(I32)
    rank = info[1:2, :]
    place = info[2:3, :]
    plane = rel_home // PLANE
    target = jnp.where(place < cap, plane * cap + place.astype(I32), -1)
    info[3:4, :] = target.astype(F32)
    over = jnp.where(jnp.max(place, axis=1, keepdims=True) >= cap, 1.0, 0.0)
    low = (rel_home - plane * PLANE + 1).astype(F32)
    row_of = iota((16, rows), 0)
    val[...] = jnp.where(row_of == 0, low, jnp.where(row_of == 1, rank, 0.0)).astype(BF16)

    for k in range(rows // 256):
        x = emb[pl.ds(k * 256, 256), :].astype(F32)
        scale = lax.rsqrt(jnp.mean(x * x, axis=-1, keepdims=True) + EPS)
        normed[pl.ds(k * 256, 256), :] = (x * scale).astype(BF16)
    meta[0:NZ] = jnp.zeros((NZ,) + meta.shape[1:], F32)

    pl.semaphore_wait(barrier, NZ - 1 + NW - 1 + NX - 1)

    def z_copy(d):
        return pltpu.make_async_remote_copy(
            src_ref=buf.at[d], dst_ref=buf.at[NZ + d], send_sem=zss.at[d], recv_sem=zrs.at[d],
            device_id={"owner": z_dev(d)}, device_id_type=MESH)

    def m_copy(d):
        return pltpu.make_async_remote_copy(
            src_ref=meta.at[d], dst_ref=meta.at[NZ + d], send_sem=mss.at[d], recv_sem=mrs.at[d],
            device_id={"owner": z_dev(d)}, device_id_type=MESH)

    def i_copy(d, e):
        return pltpu.make_async_remote_copy(
            src_ref=stage.at[d, e], dst_ref=mem.at[:, d, e], send_sem=iss.at[d, e], recv_sem=irs.at[d, e],
            device_id={"owner": w_dev(e, 1)}, device_id_type=MESH)

    def send_plane(i, _):
        d = jnp.where(i == NZ - 1, 0, z_order(i))
        pick = hot(iota((cap, rows), 0) + d * cap == info[3:4, :].astype(I32))
        buf[d] = dot(pick, normed[...]).astype(BF16)
        notes = dot_t(val[...], pick)[0:8]
        meta[d, :, 0:cap] = jnp.where(iota((8, cap), 0) == 2, over, notes)

        @pl.when(i < NZ - 1)
        def _():
            m_copy(d).start()
            z_copy(d).start()
        return 0

    lax.fori_loop(0, NZ, send_plane, 0)

    line = iota((NW * NZ * 8, 1), 0)
    v = line % 8
    code = (line // 8 % NZ) * PLANE + (line // 64) * 4
    on_s[...] = hot(jnp.where(v < 4, code + v, -1) == info[0:1, :].astype(I32))
    oc_s[...] = hot(jnp.where(v >= 4, code + v - 4, -1) == info[0:1, :].astype(I32))
    acc[...] = jnp.zeros_like(acc)
    flags[...] = jnp.zeros_like(flags)
    first = hot((iota((16, 128), 1) == 0))

    def step(j, _):
        @pl.when(j < NZ)
        def _():
            d = jnp.where(j == 0, 0, z_order(j - 1))

            @pl.when(j > 0)
            def _():
                m_copy(d).wait_recv()
                z_copy(d).wait_recv()
            slot = jnp.where(j == 0, 0, NZ + d)
            notes = meta[slot]
            q = ((notes[0:1, 0:cap] - 1.0) * RANKS + notes[1:2, 0:cap]).astype(I32)
            mark = MARK + MARK * jnp.max(notes[2:3, :], axis=1, keepdims=True)
            spread = jnp.where(iota((NW * 64, cap), 0) == q, 1.0, 0.0)
            absent = 1.0 - jnp.sum(spread, axis=1, keepdims=True)
            out = dot(spread.astype(BF16), buf[slot])
            head = out[:, 0:128] + jnp.where(iota((NW * 64, 128), 1) == 0, absent * mark, 0.0)
            stage[d, :, :, :, 0:128] = head.astype(BF16).reshape(NW, 4, RANKS, 128)
            stage[d, :, :, :, 128:] = out[:, 128:].astype(BF16).reshape(NW, 4, RANKS, feat - 128)
            mem[:, d, 0] = stage[d, 0]
            for e in range(1, NW):
                i_copy(d, e).start()

        @pl.when(j > 0)
        def _():
            d = jnp.where(j == 1, 0, z_order(j - 2))
            for e in range(1, NW):
                i_copy(d, e).wait_recv()
            for k in range(4):
                block = mem[k, d].reshape(NW * RANKS, feat)
                lead = dot_t(first, block[:, 0:128])
                flags[...] = jnp.maximum(flags[...], lead)
                acc[k] += dot(hot(lead < 64.0), block)
        return 0

    lax.fori_loop(0, NZ + 1, step, 0)

    xbuf[gx] = jnp.zeros((8, feat), F32)
    for k in range(4):
        xbuf[gx, k:k + 1, :] = acc[k, 0:1, :]
    top = jnp.max(jnp.max(flags[...], axis=0, keepdims=True), axis=1, keepdims=True)
    xbuf[gx, 4:5, :] = jnp.broadcast_to(jnp.where(top > 1.5 * MARK, 1.0, 0.0), (1, feat))

    def x_copy(k):
        return pltpu.make_async_remote_copy(
            src_ref=xbuf.at[gx], dst_ref=xbuf.at[gx], send_sem=xss.at[k], recv_sem=xrs.at[k],
            device_id={"group": lax.rem(gx + k, NX)}, device_id_type=MESH)

    def x_arrival(k):
        return pltpu.make_async_remote_copy(
            src_ref=xbuf.at[gx], dst_ref=xbuf.at[lax.rem(gx - k + NX, NX)], send_sem=xss.at[k], recv_sem=xrs.at[k],
            device_id={"group": lax.rem(gx + k, NX)}, device_id_type=MESH)

    for k in range(1, NX):
        x_copy(k).start()

    n = NZ * NW * RANKS

    def score(i, _):
        k, jb = i // 4, lax.rem(i, 4)
        every = mem[k].reshape(n, feat)
        some = mem[k, pl.ds(jb * 2, 2)].reshape(256, feat)
        s = dot_t(every, some)
        gone = every[:, 0:128].astype(F32)[:, 0:1] > 64.0
        s = s + jnp.where(gone, NEG, 0.0)
        s = jnp.where(iota((n, 256), 0) == jb * 256 + iota((n, 256), 1), NEG, s)
        best = jnp.maximum(jnp.max(s, axis=0, keepdims=True) * (1.0 / feat), -1.0)
        near[k, jb * 2] = best[:, 0:128]
        near[k, jb * 2 + 1] = best[:, 128:256]
        return 0

    lax.fori_loop(0, 16, score, 0)

    for k in range(1, NX):
        x_arrival(k).wait_recv()
    totals = ((xbuf[0] + xbuf[1]) + xbuf[2]) + xbuf[3]
    centroids = totals * lax.rsqrt(jnp.mean(totals * totals, axis=-1, keepdims=True) + EPS)
    cent_o[...] = centroids[0:4]
    flag_o[...] = jnp.broadcast_to(totals[4:5, 0:128], (8, 128))
    lowc = jnp.concatenate([centroids, centroids], axis=0).astype(BF16)
    for k in range(4):
        central = dot_t(lowc, mem[k].reshape(n, feat)) * (1.0 / feat)
        for d in range(NZ):
            ret[d, k:k + 1, :] = near[k, d]
            ret[d, 4 + k:5 + k, :] = central[k:k + 1, d * 128:(d + 1) * 128]

    def r_copy(d):
        return pltpu.make_async_remote_copy(
            src_ref=ret.at[d], dst_ref=rz.at[d], send_sem=rss.at[d], recv_sem=rrs.at[d],
            device_id={"owner": z_dev(-d)}, device_id_type=MESH)

    def p_copy(e):
        return pltpu.make_async_remote_copy(
            src_ref=rz, dst_ref=rp.at[e], send_sem=pss.at[e], recv_sem=prs.at[e],
            device_id={"owner": w_dev(e, -1)}, device_id_type=MESH)

    for d in range(1, NZ):
        r_copy(d).start()
    rz[0] = ret[0]
    for d in range(1, NZ):
        r_copy(d).wait_recv()
    for e in range(1, NW):
        p_copy(e).start()
    rp[0] = rz[...]
    for e in range(1, NW):
        p_copy(e).wait_recv()

    back = rp[...].reshape(NW * NZ * 8, 128).T
    high = back.astype(BF16)
    both = jnp.concatenate([high, (back - high.astype(F32)).astype(BF16)], axis=0)
    rel_home = info[0:1, :].astype(I32)
    lane = (rel_home % PLANE) // 4 * RANKS + info[1:2, :].astype(I32)
    mine = iota((128, rows), 0) == lane
    for table, out_ref in ((on_s, near_o), (oc_s, central_o)):
        got = dot(both, table[...])
        got = got[0:128] + got[128:256]
        out_ref[...] = jnp.sum(jnp.where(mine, got, 0.0), axis=0, keepdims=True)

    for d in range(1, NZ):
        m_copy(d).wait_send()
        z_copy(d).wait_send()
        r_copy(d).wait_send()
    for e in range(1, NW):
        p_copy(e).wait_send()
    for k in range(1, NX):
        x_copy(k).wait_send()

    def drain(d, _):
        for e in range(1, NW):
            i_copy(d, e).wait_send()
        return 0

    lax.fori_loop(0, NZ, drain, 0)


def window(cap, collective_id, embeddings, ids, home_map):
    rows, feat = embeddings.shape
    dma = pltpu.SemaphoreType.DMA
    lanes = -(-cap // 128) * 128
    vmem = pl.BlockSpec(memory_space=pltpu.VMEM)
    cent, near, central, flag = pl.pallas_call(
        functools.partial(kernel, cap),
        out_shape=(
            jax.ShapeDtypeStruct((4, feat), F32),
            jax.ShapeDtypeStruct((1, rows), F32),
            jax.ShapeDtypeStruct((1, rows), F32),
            jax.ShapeDtypeStruct((8, 128), F32),
        ),
        in_specs=[vmem] * 3,
        out_specs=(vmem,) * 4,
        scratch_shapes=[
            pltpu.VMEM((rows, feat), BF16),
            pltpu.VMEM((2 * NZ, cap, feat), BF16),
            pltpu.VMEM((2 * NZ, 8, lanes), F32),
            pltpu.VMEM((NZ, NW, 4, RANKS, feat), BF16),
            pltpu.VMEM((4, NZ, NW, RANKS, feat), BF16),
            pltpu.VMEM((8, rows), F32),
            pltpu.VMEM((16, rows), BF16),
            pltpu.VMEM((4, 16, feat), F32),
            pltpu.VMEM((16, 128), F32),
            pltpu.VMEM((NX, 8, feat), F32),
            pltpu.VMEM((4, NZ, 1, 128), F32),
            pltpu.VMEM((NZ, 8, 128), F32),
            pltpu.VMEM((NZ, 8, 128), F32),
            pltpu.VMEM((NW, NZ, 8, 128), F32),
            pltpu.VMEM((NW * NZ * 8, rows), BF16),
            pltpu.VMEM((NW * NZ * 8, rows), BF16),
            dma((NZ,)), dma((NZ,)), dma((NZ,)), dma((NZ,)),
            dma((NZ, NW)), dma((NZ, NW)),
            dma((NX,)), dma((NX,)), dma((NZ,)), dma((NZ,)), dma((NW,)), dma((NW,)),
        ],
        compiler_params=pltpu.CompilerParams(
            collective_id=collective_id, has_side_effects=True, vmem_limit_bytes=62 * 1024 * 1024),
    )(embeddings, ids, home_map)
    return cent, near.reshape(-1), central.reshape(-1), flag


def body(embeddings, assignment, home_map):
    ids = assignment.reshape(1, -1)
    table = home_map.reshape(1, -1)
    cent, near, central, flag = window(288, 0, embeddings, ids, table)
    return lax.cond(
        flag[0, 0] > 0.5,
        lambda e, i, t, *_: window(384, 1, e, i, t)[:3],
        lambda e, i, t, *done: done,
        embeddings, ids, table, cent, near, central)


def solution(mesh):
    in_specs = (P(("group", "owner"), None), P(("group", "owner"), None), P())
    out_specs = (P("owner", None), P(("group", "owner")), P(("group", "owner")))
    return jax.shard_map(body, mesh=mesh, in_specs=in_specs, out_specs=out_specs, check_vma=False)
```

time: 441 us -> 165 us (0.37); the launches traced: 435 us -> 165 us
  waiting for transfers between devices: 222 us -> 0 us
  Pallas kernels: 0 us -> 160 us
  local copies, waits for them, and re-layouts: 62.3 us -> 1.8 us
  matrix products: 58 us -> 0 us
  starting transfers between devices: 46.3 us -> 0 us
  other arithmetic: 18.3 us -> 1.24 us
  between operations: 15.1 us -> 1.33 us
  blocking collectives: 13.1 us -> 0 us
    unnamed x2 -> x0, waiting for transfers between devices: 219 us -> none
    pallas_call x0 -> x1, Pallas kernels: none -> 160 us  [window(): pl.pallas_call(functools.partial(kernel, cap), out_shape=(jax.ShapeDtypeS...]
    dot_general x3 -> x0, matrix products: 58 us -> none  [the longest x1 46.5 us: body(): jnp.einsum('acpd,bcqd->acpbq', members, members, preferred_element_type=j...]
    all_to_all x4 -> x0, starting transfers between devices: 46.3 us -> none  [the longest x1 13.5 us: body(): lax.all_to_all(slot_marks.reshape(owners, per_owner, CAP), 'owner', split...]
    reshape x5 -> x0, local copies, waits for them, and re-layouts: 31 us -> none  [the longest x2 29.9 us: body(): outgoing.reshape(owners, per_owner, CAP, feature_count)]
    gather x2 -> x0, local copies, waits for them, and re-layouts: 16.8 us -> none  [the longest x1 8.38 us: body(): nearest_rows = jnp.take(nearest_back.reshape(-1), targets)]
    psum x1 -> x0, blocking collectives: 13.1 us -> none  [body(): cluster_totals = lax.psum(own_sums, 'group')]
    scatter x1 -> x0, other arithmetic: 12 us -> none  [body(): jnp.zeros((clusters * CAP, feature_count), jnp.bfloat16).at[targets]]
  transfers between devices with their start and end apart: 5 -> 0, of which waited for: 3 -> 0; matrix products, arithmetic and copies ran while one was open for 15% -> 0% of each run, Pallas kernels for 0% -> 0%
where the time goes in v1:
time: 165 us
  Pallas kernels  160 us (97%)
  local copies, waits for them, and re-layouts  1.8 us (1%)
    pallas_call x1, Pallas kernels, window(): pl.pallas_call(functools.partial(kernel, cap), out_shape=(jax.ShapeDtypeS...  160 us

profile of v1, /device:TPU:1, one launch (start us, length us, event | category | flops | bytes accessed | tf_op | source)
XLA Modules:
  0.0 164.9 jit_solution(13919660686334771303)
XLA Ops:
  0.6 0.0 copy-start.1
  0.6 0.0 copy-start
  0.7 160.4 %shard_map.58 = (f32[4,1024]{1,0:T(4,128)S(1)}, f32[1,1536]{1,0:T(1,128)S(1)}, f32[1,1536]{1,0:T(1,128)S(1)}, f32[8,128]{1,0:T(8,128)}) custom-call(bf16[1536,1024]{1,0:T(8,128)(2,1)} %emb.1, s32[1,1536]{1,0:T(1,128)} %bitcast.3, s32[1,256]{1,0:T(1,128)} %bitcast.5), custom_call_target="tpu_custom_call" | custom-call | tf_op jit(solution)/shard_map/pallas_call | solution.py:285
  161.0 1.2 slice.3
  162.9 0.0 copy-done.1
  162.9 0.0 copy-done
  162.9 0.2 conditional.1
  163.1 0.6 reduce.1
  163.7 0.6 reduce
  164.3 0.6 copy.13
Async XLA Ops:
  0.6 162.2 %copy-start.1 = (s32[256]{0:T(256)S(1)}, s32[256]{0:T(256)}, u32[]{:S(2)}) copy-start(s32[256]{0:T(256)} %param.7) | copy-start | bytes 3076
  0.6 162.2 %copy-start = (s32[1536,1]{0,1:T(1,128)S(1)}, s32[1536,1]{0,1:T(1,128)}, u32[]{:S(2)}) copy-start(s32[1536,1]{0,1:T(1,128)} %param.6) | copy-start | bytes 18436

commit v2 on v1

v2 whole, which is shorter than its diff:
```python
import functools

import jax
import jax.numpy as jnp
from jax import lax
from jax.experimental import pallas as pl
from jax.experimental.pallas import tpu as pltpu
from jax.sharding import PartitionSpec as P

MESH = pl.DeviceIdType.MESH
F32 = jnp.float32
BF16 = jnp.bfloat16
I32 = jnp.int32

NZ, NY, NC = 8, 4, 2
NW = NY * NC
NX = 4
PLANE = 32
RANKS = 16
MARK = 128.0
NEG = -1e30
EPS = 1e-06
HALVES = 2
CAP = 272


def dot(a, b):
    return lax.dot_general(a, b, (((1,), (0,)), ((), ())), preferred_element_type=F32)


def dot_t(a, b):
    return lax.dot_general(a, b, (((1,), (1,)), ((), ())), preferred_element_type=F32)


def iota(shape, axis):
    return lax.broadcasted_iota(I32, shape, axis)


def hot(mask):
    return jnp.where(mask, 1.0, 0.0).astype(BF16)


def z_of(j):
    return jnp.where(lax.rem(j, 2) == 1, (j + 1) // 2, NZ - j // 2)


def kernel(cap, emb_hbm, ids, hm, cent_o, near_o, central_o, flag_o,
           emb, buf, meta, stage, mem, info, val, acc, flags, xbuf, near, ret, rz, pk, rp, on_s, oc_s,
           esem, zss, zrs, mss, mrs, iss, irs, xss, xrs, rss, rrs, pss, prs):
    rows, feat = emb.shape
    half = feat // HALVES
    clusters = hm.shape[1]
    gx = lax.axis_index("group")
    me = lax.axis_index("owner")
    z, y, c = me // NW, lax.rem(me // NC, NY), lax.rem(me, NC)

    def z_dev(j, sign=1):
        return lax.rem(z + sign * z_of(j) + NZ, NZ) * NW + y * NC + c

    def w_dev(e, sign):
        dy, dc = e // NC, lax.rem(e, NC)
        return z * NW + lax.rem(y + sign * dy + NY, NY) * NC + lax.rem(c + dc, NC)

    barrier = pltpu.get_barrier_semaphore()
    for j in range(1, NZ):
        pl.semaphore_signal(barrier, inc=1, device_id={"owner": z_dev(j)}, device_id_type=MESH)
    for e in range(1, NW):
        pl.semaphore_signal(barrier, inc=1, device_id={"owner": w_dev(e, 1)}, device_id_type=MESH)
    for k in range(1, NX):
        pl.semaphore_signal(barrier, inc=1, device_id={"group": lax.rem(gx + k, NX)}, device_id_type=MESH)
    load = pltpu.make_async_copy(emb_hbm, emb, esem)
    load.start()

    h = hm[...]
    dz = ((h >> 5) - z) & (NZ - 1)
    jz = jnp.where(dz == 0, 0, jnp.where(dz <= NZ // 2, 2 * dz - 1, 2 * (NZ - dz)))
    rel = (jz << 5) + ((((h >> 3) - y) & (NY - 1)) << 3) + ((((h >> 2) - c) & 1) << 2) + (h & 3)
    perm = hot(iota((clusters, clusters), 0) == rel)
    home = dot(perm, hot(iota((clusters, rows), 0) == ids[...])).astype(BF16)
    before = hot(iota((256, 256), 0) < iota((256, 256), 1))
    same = hot((iota((clusters, clusters), 0) >> 5) == (iota((clusters, clusters), 1) >> 5))
    base = jnp.zeros((clusters, 1), F32)
    number = iota((clusters, 256), 0).astype(F32)
    for k in range(rows // 256):
        part = home[:, k * 256:(k + 1) * 256]
        count = dot(part, before) + base
        wide = part.astype(F32)
        lanes = pl.ds(k * 256, 256)
        info[0:1, lanes] = jnp.sum(wide * number, axis=0, keepdims=True)
        info[1:2, lanes] = jnp.sum(wide * count, axis=0, keepdims=True)
        info[2:3, lanes] = jnp.sum(dot(same, part) * count, axis=0, keepdims=True)
        base = base + jnp.sum(wide, axis=1, keepdims=True)
    rel_home = info[0:1, :].astype(I32)
    rank = info[1:2, :]
    place = info[2:3, :]
    plane = rel_home >> 5
    low = rel_home & (PLANE - 1)
    info[3:4, :] = jnp.where(place < cap, plane * cap + place.astype(I32), -1).astype(F32)
    over = jnp.where(jnp.max(place, axis=1, keepdims=True) >= cap, 1.0, 0.0)
    row_of = iota((16, rows), 0)
    val[...] = jnp.where(row_of == 0, (low + 1).astype(F32), jnp.where(row_of == 1, rank, 0.0)).astype(BF16)
    lanes = meta.shape[2]
    if lanes > cap:
        meta[0:NZ] = jnp.zeros((NZ, 8, lanes), F32)

    pl.semaphore_wait(barrier, NZ - 1 + NW - 1 + NX - 1)
    load.wait()

    def z_copy(j, f):
        return pltpu.make_async_remote_copy(
            src_ref=buf.at[j, f], dst_ref=buf.at[NZ + j, f], send_sem=zss.at[j, f], recv_sem=zrs.at[j, f],
            device_id={"owner": z_dev(j)}, device_id_type=MESH)

    def m_copy(j):
        return pltpu.make_async_remote_copy(
            src_ref=meta.at[j], dst_ref=meta.at[NZ + j], send_sem=mss.at[j], recv_sem=mrs.at[j],
            device_id={"owner": z_dev(j)}, device_id_type=MESH)

    def i_copy(j, f, e):
        return pltpu.make_async_remote_copy(
            src_ref=stage.at[j, f, e], dst_ref=mem.at[:, j, e, :, pl.ds(f * half, half)],
            send_sem=iss.at[j, f, e], recv_sem=irs.at[j, f, e],
            device_id={"owner": w_dev(e, 1)}, device_id_type=MESH)

    def send_plane(i, _):
        j = lax.rem(i + 1, NZ)
        pick = hot(iota((cap, rows), 0) + j * cap == info[3:4, :].astype(I32))
        x = dot(pick, emb[...])
        x = x * lax.rsqrt(jnp.mean(x * x, axis=-1, keepdims=True) + EPS)
        for f in range(HALVES):
            buf[j, f] = x[:, f * half:(f + 1) * half].astype(BF16)
        notes = dot_t(val[...], pick)[0:8]
        meta[j, :, 0:cap] = jnp.where(iota((8, cap), 0) == 2, over, notes)

        @pl.when(j > 0)
        def _():
            m_copy(j).start()
            for f in range(HALVES):
                z_copy(j, f).start()
        return 0

    lax.fori_loop(0, NZ, send_plane, 0)

    line = iota((128, 1), 0)
    v = line & 7
    code = (line >> 3) * 4
    low = info[0:1, :].astype(I32) & (PLANE - 1)
    on_s[...] = hot(jnp.where((v < 4) & (line < 64), code + v, -1) == low)
    oc_s[...] = hot(jnp.where((v >= 4) & (line < 64), code + v - 4, -1) == low)
    acc[...] = jnp.zeros_like(acc)
    flags[...] = jnp.zeros_like(flags)
    first = hot((iota((16, 128), 1) == 0))

    def collect(j):
        for e in range(1, NW):
            for f in range(HALVES):
                i_copy(j, f, e).wait_recv()
        for k in range(4):
            block = mem[k, j].reshape(NW * RANKS, feat)
            lead = dot_t(first, block[:, 0:128])
            flags[...] = jnp.maximum(flags[...], lead)
            acc[k] += dot(hot(lead < 64.0), block)

    def step(j, _):
        @pl.when(j > 0)
        def _():
            m_copy(j).wait_recv()
        slot = jnp.where(j == 0, 0, NZ + j)
        notes = meta[slot]
        q = ((notes[0:1, 0:cap] - 1.0) * RANKS + notes[1:2, 0:cap]).astype(I32)
        mark = MARK + MARK * jnp.max(notes[2:3, 0:cap], axis=1, keepdims=True)
        spread = jnp.where(iota((NW * 64, cap), 0) == q, 1.0, 0.0)
        absent = 1.0 - jnp.sum(spread, axis=1, keepdims=True)
        head = jnp.where(iota((NW * 64, 128), 1) == 0, absent * mark, 0.0)
        spread = spread.astype(BF16)
        for f in range(HALVES):
            @pl.when(j > 0)
            def _():
                z_copy(j, f).wait_recv()
            out = dot(spread, buf[slot, f])
            if f == 0:
                stage[j, f, :, :, :, 0:128] = (out[:, 0:128] + head).astype(BF16).reshape(NW, 4, RANKS, 128)
                stage[j, f, :, :, :, 128:] = out[:, 128:].astype(BF16).reshape(NW, 4, RANKS, half - 128)
            else:
                stage[j, f] = out.astype(BF16).reshape(NW, 4, RANKS, half)
            for e in range(1, NW):
                i_copy(j, f, e).start()
            mem[:, j, 0, :, f * half:(f + 1) * half] = stage[j, f, 0]

        @pl.when(j > 0)
        def _():
            collect(j - 1)
        return 0

    lax.fori_loop(0, NZ, step, 0)

    n = NZ * NW * RANKS
    group = NW * RANKS
    early = n - group

    def gone(block):
        return jnp.where(block[:, 0:128].astype(F32)[:, 0:1] > 64.0, NEG, 0.0)

    def score(k, _):
        every = mem[k, 0:NZ - 1].reshape(early, feat)
        s = dot_t(every, every) + gone(every)
        s = jnp.where(iota((early, early), 0) == iota((early, early), 1), NEG, s)
        near[k, :, 0:early] = jnp.max(s, axis=0, keepdims=True)
        return 0

    lax.fori_loop(0, 4, score, 0)
    collect(NZ - 1)

    xbuf[gx] = jnp.zeros((8, feat), F32)
    for k in range(4):
        xbuf[gx, k:k + 1, :] = acc[k, 0:1, :]
    top = jnp.max(jnp.max(flags[...], axis=0, keepdims=True), axis=1, keepdims=True)
    xbuf[gx, 4:5, :] = jnp.broadcast_to(jnp.where(top > 1.5 * MARK, 1.0, 0.0), (1, feat))

    def x_copy(k, place):
        return pltpu.make_async_remote_copy(
            src_ref=xbuf.at[gx], dst_ref=xbuf.at[place], send_sem=xss.at[k], recv_sem=xrs.at[k],
            device_id={"group": lax.rem(gx + k, NX)}, device_id_type=MESH)

    for k in range(1, NX):
        x_copy(k, gx).start()

    def score_last(k, _):
        every = mem[k].reshape(n, feat)
        last = every[early:]
        s = dot_t(every, last) + gone(every)
        s = jnp.where(iota((n, group), 0) == early + iota((n, group), 1), NEG, s)
        near[k, :, early:n] = jnp.max(s, axis=0, keepdims=True)
        s = dot_t(last, every[0:early]) + gone(last)
        near[k, :, 0:early] = jnp.maximum(near[k, :, 0:early], jnp.max(s, axis=0, keepdims=True))
        return 0

    lax.fori_loop(0, 4, score_last, 0)

    for k in range(1, NX):
        x_copy(k, lax.rem(gx - k + NX, NX)).wait_recv()
    totals = ((xbuf[0] + xbuf[1]) + xbuf[2]) + xbuf[3]
    centroids = totals * lax.rsqrt(jnp.mean(totals * totals, axis=-1, keepdims=True) + EPS)
    cent_o[...] = centroids[0:4]
    flag_o[...] = jnp.broadcast_to(totals[4:5, 0:128], (8, 128))
    lowc = jnp.concatenate([centroids, centroids], axis=0).astype(BF16)
    for k in range(4):
        central = dot_t(lowc, mem[k].reshape(n, feat)) * (1.0 / feat)
        nearest = jnp.maximum(near[k] * (1.0 / feat), -1.0)
        for j in range(NZ):
            ret[j, k:k + 1, :] = nearest[:, j * 128:(j + 1) * 128]
            ret[j, 4 + k:5 + k, :] = central[k:k + 1, j * 128:(j + 1) * 128]

    def r_copy(j):
        return pltpu.make_async_remote_copy(
            src_ref=ret.at[j], dst_ref=rz.at[j], send_sem=rss.at[j], recv_sem=rrs.at[j],
            device_id={"owner": z_dev(j, -1)}, device_id_type=MESH)

    def p_copy(e):
        return pltpu.make_async_remote_copy(
            src_ref=pk.at[e], dst_ref=rp.at[e], send_sem=pss.at[e], recv_sem=prs.at[e],
            device_id={"owner": w_dev(e, -1)}, device_id_type=MESH)

    for j in range(1, NZ):
        r_copy(j).start()
    rz[0] = ret[0]
    rp[NW:] = jnp.zeros((NW, 8, 128), F32)
    for j in range(1, NZ):
        r_copy(j).wait_recv()
    got = [rz[j] for j in range(NZ)]
    block = iota((8, 128), 1) >> 4
    for e in range(NW):
        out = jnp.zeros((8, 128), F32)
        for j in range(NZ):
            shift = (j - e) % NZ * RANKS
            out = jnp.where(block == j, pltpu.roll(got[j], shift, 1) if shift else got[j], out)
        if e == 0:
            rp[0] = out
        else:
            pk[e] = out
            p_copy(e).start()
    for e in range(1, NW):
        p_copy(e).wait_recv()

    back = rp[...].reshape(128, 128).T
    high = back.astype(BF16)
    both = jnp.concatenate([high, (back - high.astype(F32)).astype(BF16)], axis=0)
    lane = (info[0:1, :].astype(I32) >> 5) * RANKS + info[1:2, :].astype(I32)
    mine = iota((128, rows), 0) == lane
    for table, out_ref in ((on_s, near_o), (oc_s, central_o)):
        took = dot(both, table[...])
        took = jnp.sum(jnp.where(mine, took[0:128] + took[128:256], 0.0), axis=0, keepdims=True)
        for k in range(rows // 128):
            out_ref[k:k + 1, :] = took[:, k * 128:(k + 1) * 128]

    for j in range(1, NZ):
        m_copy(j).wait_send()
        for f in range(HALVES):
            z_copy(j, f).wait_send()
        r_copy(j).wait_send()
    for e in range(1, NW):
        p_copy(e).wait_send()
    for k in range(1, NX):
        x_copy(k, gx).wait_send()

    def drain(j, _):
        for e in range(1, NW):
            for f in range(HALVES):
                i_copy(j, f, e).wait_send()
        return 0

    lax.fori_loop(0, NZ, drain, 0)


def window(cap, collective_id, embeddings, ids, home_map):
    rows, feat = embeddings.shape
    dma = pltpu.SemaphoreType.DMA
    lanes = -(-cap // 128) * 128
    vmem = pl.BlockSpec(memory_space=pltpu.VMEM)
    cent, near, central, flag = pl.pallas_call(
        functools.partial(kernel, cap),
        out_shape=(
            jax.ShapeDtypeStruct((4, feat), F32),
            jax.ShapeDtypeStruct((rows // 128, 128), F32),
            jax.ShapeDtypeStruct((rows // 128, 128), F32),
            jax.ShapeDtypeStruct((8, 128), F32),
        ),
        in_specs=[pl.BlockSpec(memory_space=pl.ANY), vmem, vmem],
        out_specs=(vmem,) * 4,
        scratch_shapes=[
            pltpu.VMEM((rows, feat), BF16),
            pltpu.VMEM((2 * NZ, HALVES, cap, feat // HALVES), BF16),
            pltpu.VMEM((2 * NZ, 8, lanes), F32),
            pltpu.VMEM((NZ, HALVES, NW, 4, RANKS, feat // HALVES), BF16),
            pltpu.VMEM((4, NZ, NW, RANKS, feat), BF16),
            pltpu.VMEM((8, rows), F32),
            pltpu.VMEM((16, rows), BF16),
            pltpu.VMEM((4, 16, feat), F32),
            pltpu.VMEM((16, 128), F32),
            pltpu.VMEM((NX, 8, feat), F32),
            pltpu.VMEM((4, 1, NZ * NW * RANKS), F32),
            pltpu.VMEM((NZ, 8, 128), F32),
            pltpu.VMEM((NZ, 8, 128), F32),
            pltpu.VMEM((NW, 8, 128), F32),
            pltpu.VMEM((2 * NW, 8, 128), F32),
            pltpu.VMEM((128, rows), BF16),
            pltpu.VMEM((128, rows), BF16),
            dma, dma((NZ, HALVES)), dma((NZ, HALVES)), dma((NZ,)), dma((NZ,)),
            dma((NZ, HALVES, NW)), dma((NZ, HALVES, NW)),
            dma((NX,)), dma((NX,)), dma((NZ,)), dma((NZ,)), dma((NW,)), dma((NW,)),
        ],
        compiler_params=pltpu.CompilerParams(
            collective_id=collective_id, has_side_effects=True, vmem_limit_bytes=62 * 1024 * 1024),
    )(embeddings, ids, home_map)
    return cent, near.reshape(-1), central.reshape(-1), flag


def body(embeddings, assignment, home_map):
    ids = assignment.reshape(1, -1)
    table = home_map.reshape(1, -1)
    cent, near, central, flag = window(CAP, 0, embeddings, ids, table)
    return lax.cond(
        flag[0, 0] > 0.5,
        lambda e, i, t, *_: window(PLANE * 12, 1, e, i, t)[:3],
        lambda e, i, t, *done: done,
        embeddings, ids, table, cent, near, central)


def solution(mesh):
    in_specs = (P(("group", "owner"), None), P(("group", "owner"), None), P())
    out_specs = (P("owner", None), P(("group", "owner")), P(("group", "owner")))
    return jax.shard_map(body, mesh=mesh, in_specs=in_specs, out_specs=out_specs, check_vma=False)
```

time: 165 us -> 149 us (0.903)
  Pallas kernels: 160 us -> 144 us
    pallas_call x1, Pallas kernels: 160 us -> 144 us  [window(): pl.pallas_call(functools.partial(kernel, cap), out_shape=(jax.ShapeDtypeS...]
where the time goes in v2:
time: 149 us
  Pallas kernels  144 us (97%)
  local copies, waits for them, and re-layouts  3.01 us (2%)
    pallas_call x1, Pallas kernels, window(): pl.pallas_call(functools.partial(kernel, cap), out_shape=(jax.ShapeDtypeS...  144 us

profile of v2, /device:TPU:1, one launch (start us, length us, event | category | flops | bytes accessed | tf_op | source)
XLA Modules:
  0.0 148.8 jit_solution(3256307215897234365)
XLA Ops:
  0.6 0.0 copy-start.1
  0.6 0.0 copy-start
  0.7 144.3 %shard_map.58 = (f32[4,1024]{1,0:T(4,128)S(1)}, f32[12,128]{1,0:T(8,128)S(1)}, f32[12,128]{1,0:T(8,128)S(1)}, f32[8,128]{1,0:T(8,128)}) custom-call(bf16[1536,1024]{1,0:T(8,128)(2,1)} %emb_hbm.1, s32[1,1536]{1,0:T(1,128)} %bitcast.5, s32[1,256]{1,0:T(1,128)} %bitcast.9), custom_call_target="tpu_custom_call" | custom-call | tf_op jit(solution)/shard_map/pallas_call | solution.py:320
  144.9 1.2 slice.3
  146.8 0.0 copy-done.1
  146.8 0.0 copy-done
  146.8 0.2 conditional.1
  147.0 0.6 copy.15
  147.6 0.6 copy.16
  148.2 0.6 copy.17
Async XLA Ops:
  0.6 146.2 %copy-start.1 = (s32[256]{0:T(256)S(1)}, s32[256]{0:T(256)}, u32[]{:S(2)}) copy-start(s32[256]{0:T(256)} %param.7) | copy-start | bytes 3076
  0.6 146.2 %copy-start = (s32[1536,1]{0,1:T(1,128)S(1)}, s32[1536,1]{0,1:T(1,128)}, u32[]{:S(2)}) copy-start(s32[1536,1]{0,1:T(1,128)} %param.6) | copy-start | bytes 18436

commit v3 on v2

--- a/solution.py
+++ b/solution.py
@@ -45,8 +45,8 @@
 
 
 def kernel(cap, emb_hbm, ids, hm, cent_o, near_o, central_o, flag_o,
-           emb, buf, meta, stage, mem, info, val, acc, flags, xbuf, near, ret, rz, pk, rp, on_s, oc_s,
-           esem, zss, zrs, mss, mrs, iss, irs, xss, xrs, rss, rrs, pss, prs):
+           emb, cent_v, near_v, central_v, head, spr, sel, buf, meta, stage, mem, info, val, acc, flags, xbuf, near, ret, rz, pk, rp, on_s, oc_s,
+           esem, osem, zss, zrs, mss, mrs, iss, irs, xss, xrs, rss, rrs, pss, prs):
     rows, feat = emb.shape
     half = feat // HALVES
     clusters = hm.shape[1]
@@ -94,16 +94,19 @@
     rank = info[1:2, :]
     place = info[2:3, :]
     plane = rel_home >> 5
-    low = rel_home & (PLANE - 1)
+    e4 = rel_home & (PLANE - 1)
+    irank = rank.astype(I32)
+    own = (e4 & 3) < 3
+    tile = (e4 >> 2) * 3 + jnp.where(own, e4 & 3, irank >> 2)
+    row = jnp.where(own, irank, 12 + (irank & 3))
     info[3:4, :] = jnp.where(place < cap, plane * cap + place.astype(I32), -1).astype(F32)
     over = jnp.where(jnp.max(place, axis=1, keepdims=True) >= cap, 1.0, 0.0)
     row_of = iota((16, rows), 0)
-    val[...] = jnp.where(row_of == 0, (low + 1).astype(F32), jnp.where(row_of == 1, rank, 0.0)).astype(BF16)
+    val[...] = jnp.where(row_of == 0, tile + 1, jnp.where(row_of == 1, row, 0)).astype(F32).astype(BF16)
     lanes = meta.shape[2]
     if lanes > cap:
         meta[0:NZ] = jnp.zeros((NZ, 8, lanes), F32)
 
-    pl.semaphore_wait(barrier, NZ - 1 + NW - 1 + NX - 1)
     load.wait()
 
     def z_copy(j, f):
@@ -118,7 +121,7 @@
 
     def i_copy(j, f, e):
         return pltpu.make_async_remote_copy(
-            src_ref=stage.at[j, f, e], dst_ref=mem.at[:, j, e, :, pl.ds(f * half, half)],
+            src_ref=stage.at[j, f, e], dst_ref=mem.at[0:3, j, e, :, pl.ds(f * half, half)],
             send_sem=iss.at[j, f, e], recv_sem=irs.at[j, f, e],
             device_id={"owner": w_dev(e, 1)}, device_id_type=MESH)
 
@@ -132,6 +135,10 @@
         notes = dot_t(val[...], pick)[0:8]
         meta[j, :, 0:cap] = jnp.where(iota((8, cap), 0) == 2, over, notes)
 
+        @pl.when(i == 0)
+        def _():
+            pl.semaphore_wait(barrier, NZ - 1 + NW - 1 + NX - 1)
+
         @pl.when(j > 0)
         def _():
             m_copy(j).start()
@@ -151,55 +158,69 @@
     flags[...] = jnp.zeros_like(flags)
     first = hot((iota((16, 128), 1) == 0))
 
+    group = NW * RANKS
+    to = iota((group, 3 * group), 0)
+    at = iota((group, 3 * group), 1)
+    sel[...] = hot(at == ((to & 15) >> 2) * group + (to & ~15) + 12 + (to & 3))
+
     def collect(j):
         for e in range(1, NW):
             for f in range(HALVES):
                 i_copy(j, f, e).wait_recv()
+        tiles = mem[0:3, j].reshape(3 * group, feat)
+        mem[3, j] = dot(sel[...], tiles).astype(BF16).reshape(NW, RANKS, feat)
+        used = (iota((16, group), 1) & 15) < 12
         for k in range(4):
-            block = mem[k, j].reshape(NW * RANKS, feat)
+            block = mem[k, j].reshape(group, feat)
             lead = dot_t(first, block[:, 0:128])
             flags[...] = jnp.maximum(flags[...], lead)
-            acc[k] += dot(hot(lead < 64.0), block)
+            acc[k] += dot(hot((lead < 64.0) & used), block)
+
+    def spread(j, slot):
+        notes = meta[slot]
+        q = ((notes[0:1, 0:cap] - 1.0) * RANKS + notes[1:2, 0:cap]).astype(I32)
+        mark = MARK + MARK * jnp.max(notes[2:3, 0:cap], axis=1, keepdims=True)
+        wide = jnp.where(iota((NW * 48, cap), 0) == q, 1.0, 0.0)
+        absent = 1.0 - jnp.sum(wide, axis=1, keepdims=True)
+        head[...] = jnp.where(iota((NW * 48, 128), 1) == 0, absent * mark, 0.0)
+        spr[...] = wide.astype(BF16)
+
+    def piece(j, slot, f):
+        out = dot(spr[...], buf[slot, f])
+        if f == 0:
+            stage[j, f, :, :, :, 0:128] = (out[:, 0:128] + head[...]).astype(BF16).reshape(NW, 3, RANKS, 128)
+            stage[j, f, :, :, :, 128:] = out[:, 128:].astype(BF16).reshape(NW, 3, RANKS, half - 128)
+        else:
+            stage[j, f] = out.astype(BF16).reshape(NW, 3, RANKS, half)
+        for e in range(1, NW):
+            i_copy(j, f, e).start()
+        mem[0:3, j, 0, :, f * half:(f + 1) * half] = stage[j, f, 0]
 
     def step(j, _):
         @pl.when(j > 0)
         def _():
             m_copy(j).wait_recv()
         slot = jnp.where(j == 0, 0, NZ + j)
-        notes = meta[slot]
-        q = ((notes[0:1, 0:cap] - 1.0) * RANKS + notes[1:2, 0:cap]).astype(I32)
-        mark = MARK + MARK * jnp.max(notes[2:3, 0:cap], axis=1, keepdims=True)
-        spread = jnp.where(iota((NW * 64, cap), 0) == q, 1.0, 0.0)
-        absent = 1.0 - jnp.sum(spread, axis=1, keepdims=True)
-        head = jnp.where(iota((NW * 64, 128), 1) == 0, absent * mark, 0.0)
-        spread = spread.astype(BF16)
+        spread(j, slot)
         for f in range(HALVES):
             @pl.when(j > 0)
             def _():
                 z_copy(j, f).wait_recv()
-            out = dot(spread, buf[slot, f])
-            if f == 0:
-                stage[j, f, :, :, :, 0:128] = (out[:, 0:128] + head).astype(BF16).reshape(NW, 4, RANKS, 128)
-                stage[j, f, :, :, :, 128:] = out[:, 128:].astype(BF16).reshape(NW, 4, RANKS, half - 128)
-            else:
-                stage[j, f] = out.astype(BF16).reshape(NW, 4, RANKS, half)
-            for e in range(1, NW):
-                i_copy(j, f, e).start()
-            mem[:, j, 0, :, f * half:(f + 1) * half] = stage[j, f, 0]
+            piece(j, slot, f)
 
         @pl.when(j > 0)
         def _():
             collect(j - 1)
         return 0
 
-    lax.fori_loop(0, NZ, step, 0)
-
-    n = NZ * NW * RANKS
-    group = NW * RANKS
+    lax.fori_loop(0, NZ - 1, step, 0)
+
+    n = NZ * group
     early = n - group
 
     def gone(block):
-        return jnp.where(block[:, 0:128].astype(F32)[:, 0:1] > 64.0, NEG, 0.0)
+        empty = block[:, 0:128].astype(F32)[:, 0:1] > 64.0
+        return jnp.where(empty | ((iota((block.shape[0], 1), 0) & 15) >= 12), NEG, 0.0)
 
     def score(k, _):
         every = mem[k, 0:NZ - 1].reshape(early, feat)
@@ -208,8 +229,17 @@
         near[k, :, 0:early] = jnp.max(s, axis=0, keepdims=True)
         return 0
 
-    lax.fori_loop(0, 4, score, 0)
-    collect(NZ - 1)
+    last_j = NZ - 1
+    m_copy(last_j).wait_recv()
+    spread(last_j, NZ + last_j)
+    for f in range(HALVES):
+        if f == HALVES - 1:
+            collect(last_j - 1)
+            lax.fori_loop(0, 2, score, 0)
+        z_copy(last_j, f).wait_recv()
+        piece(last_j, NZ + last_j, f)
+    lax.fori_loop(2, 4, score, 0)
+    collect(last_j)
 
     xbuf[gx] = jnp.zeros((8, feat), F32)
     for k in range(4):
@@ -241,8 +271,10 @@
         x_copy(k, lax.rem(gx - k + NX, NX)).wait_recv()
     totals = ((xbuf[0] + xbuf[1]) + xbuf[2]) + xbuf[3]
     centroids = totals * lax.rsqrt(jnp.mean(totals * totals, axis=-1, keepdims=True) + EPS)
-    cent_o[...] = centroids[0:4]
-    flag_o[...] = jnp.broadcast_to(totals[4:5, 0:128], (8, 128))
+    cent_v[...] = centroids[0:4]
+    cent_out = pltpu.make_async_copy(cent_v, cent_o, osem.at[0])
+    cent_out.start()
+    flag_o[0, 0] = jnp.max(totals[4:5, 0:128]).astype(I32)
     lowc = jnp.concatenate([centroids, centroids], axis=0).astype(BF16)
     for k in range(4):
         central = dot_t(lowc, mem[k].reshape(n, feat)) * (1.0 / feat)
@@ -287,11 +319,14 @@
     both = jnp.concatenate([high, (back - high.astype(F32)).astype(BF16)], axis=0)
     lane = (info[0:1, :].astype(I32) >> 5) * RANKS + info[1:2, :].astype(I32)
     mine = iota((128, rows), 0) == lane
-    for table, out_ref in ((on_s, near_o), (oc_s, central_o)):
+    outs = [cent_out]
+    for table, out_v, out_ref in ((on_s, near_v, near_o), (oc_s, central_v, central_o)):
         took = dot(both, table[...])
         took = jnp.sum(jnp.where(mine, took[0:128] + took[128:256], 0.0), axis=0, keepdims=True)
         for k in range(rows // 128):
-            out_ref[k:k + 1, :] = took[:, k * 128:(k + 1) * 128]
+            out_v[k:k + 1, :] = took[:, k * 128:(k + 1) * 128]
+        outs.append(pltpu.make_async_copy(out_v, out_ref, osem.at[len(outs)]))
+        outs[-1].start()
 
     for j in range(1, NZ):
         m_copy(j).wait_send()
@@ -310,6 +345,8 @@
         return 0
 
     lax.fori_loop(0, NZ, drain, 0)
+    for out in outs:
+        out.wait()
 
 
 def window(cap, collective_id, embeddings, ids, home_map):
@@ -323,15 +360,21 @@
             jax.ShapeDtypeStruct((4, feat), F32),
             jax.ShapeDtypeStruct((rows // 128, 128), F32),
             jax.ShapeDtypeStruct((rows // 128, 128), F32),
-            jax.ShapeDtypeStruct((8, 128), F32),
+            jax.ShapeDtypeStruct((1, 1), I32),
         ),
         in_specs=[pl.BlockSpec(memory_space=pl.ANY), vmem, vmem],
-        out_specs=(vmem,) * 4,
+        out_specs=(pl.BlockSpec(memory_space=pltpu.HBM),) * 3 + (pl.BlockSpec(memory_space=pltpu.SMEM),),
         scratch_shapes=[
             pltpu.VMEM((rows, feat), BF16),
+            pltpu.VMEM((4, feat), F32),
+            pltpu.VMEM((rows // 128, 128), F32),
+            pltpu.VMEM((rows // 128, 128), F32),
+            pltpu.VMEM((NW * 48, 128), F32),
+            pltpu.VMEM((NW * 48, cap), BF16),
+            pltpu.VMEM((NW * RANKS, 3 * NW * RANKS), BF16),
             pltpu.VMEM((2 * NZ, HALVES, cap, feat // HALVES), BF16),
             pltpu.VMEM((2 * NZ, 8, lanes), F32),
-            pltpu.VMEM((NZ, HALVES, NW, 4, RANKS, feat // HALVES), BF16),
+            pltpu.VMEM((NZ, HALVES, NW, 3, RANKS, feat // HALVES), BF16),
             pltpu.VMEM((4, NZ, NW, RANKS, feat), BF16),
             pltpu.VMEM((8, rows), F32),
             pltpu.VMEM((16, rows), BF16),
@@ -345,7 +388,7 @@
             pltpu.VMEM((2 * NW, 8, 128), F32),
             pltpu.VMEM((128, rows), BF16),
             pltpu.VMEM((128, rows), BF16),
-            dma, dma((NZ, HALVES)), dma((NZ, HALVES)), dma((NZ,)), dma((NZ,)),
+            dma, dma((3,)), dma((NZ, HALVES)), dma((NZ, HALVES)), dma((NZ,)), dma((NZ,)),
             dma((NZ, HALVES, NW)), dma((NZ, HALVES, NW)),
             dma((NX,)), dma((NX,)), dma((NZ,)), dma((NZ,)), dma((NW,)), dma((NW,)),
         ],
@@ -360,7 +403,7 @@
     table = home_map.reshape(1, -1)
     cent, near, central, flag = window(CAP, 0, embeddings, ids, table)
     return lax.cond(
-        flag[0, 0] > 0.5,
+        flag.reshape(()) > 0,
         lambda e, i, t, *_: window(PLANE * 12, 1, e, i, t)[:3],
         lambda e, i, t, *done: done,
         embeddings, ids, table, cent, near, central)

time: 149 us -> 143 us (0.960)
  Pallas kernels: 144 us -> 140 us
    pallas_call x1, Pallas kernels: 144 us -> 140 us  [window(): pl.pallas_call(functools.partial(kernel, cap), out_shape=(jax.ShapeDtypeS...]
where the time goes in v3:
time: 143 us
  Pallas kernels  140 us (98%)
  local copies, waits for them, and re-layouts  1.81 us (1%)
    pallas_call x1, Pallas kernels, window(): pl.pallas_call(functools.partial(kernel, cap), out_shape=(jax.ShapeDtypeS...  140 us

profile of v3, /device:TPU:1, one launch (start us, length us, event | category | flops | bytes accessed | tf_op | source)
XLA Modules:
  0.0 143.0 jit_solution(9315830401717278528)
XLA Ops:
  0.6 0.0 copy-start.1
  0.6 0.0 copy-start
  0.7 139.6 %shard_map.58 = (f32[4,1024]{1,0:T(4,128)S(1)}, f32[12,128]{1,0:T(8,128)S(1)}, f32[12,128]{1,0:T(8,128)S(1)}, s32[1,1]{1,0:T(1,128)}) custom-call(bf16[1536,1024]{1,0:T(8,128)(2,1)} %emb_hbm.1, s32[1,1536]{1,0:T(1,128)} %bitcast.5, s32[1,256]{1,0:T(1,128)} %bitcast.9), custom_call_target="tpu_custom_call" | custom-call | tf_op jit(solution)/shard_map/pallas_call | solution.py:357
  140.9 0.0 copy-done.1
  140.9 0.0 copy-done
  140.9 0.2 conditional.1
  141.2 0.6 copy.15
  141.8 0.6 copy.16
  142.4 0.6 copy.17
Async XLA Ops:
  0.6 140.3 %copy-start.1 = (s32[256]{0:T(256)S(1)}, s32[256]{0:T(256)}, u32[]{:S(2)}) copy-start(s32[256]{0:T(256)} %param.7) | copy-start | bytes 3076
  0.6 140.3 %copy-start = (s32[1536,1]{0,1:T(1,128)S(1)}, s32[1536,1]{0,1:T(1,128)}, u32[]{:S(2)}) copy-start(s32[1536,1]{0,1:T(1,128)} %param.6) | copy-start | bytes 18436

commit v4 on v3

--- a/solution.py
+++ b/solution.py
@@ -20,7 +20,8 @@
 MARK = 128.0
 NEG = -1e30
 EPS = 1e-06
-HALVES = 2
+CUTS = ((0, 512), (512, 512))
+HALVES = len(CUTS)
 CAP = 272
 
 
@@ -45,10 +46,9 @@
 
 
 def kernel(cap, emb_hbm, ids, hm, cent_o, near_o, central_o, flag_o,
-           emb, cent_v, near_v, central_v, head, spr, sel, buf, meta, stage, mem, info, val, acc, flags, xbuf, near, ret, rz, pk, rp, on_s, oc_s,
-           esem, osem, zss, zrs, mss, mrs, iss, irs, xss, xrs, rss, rrs, pss, prs):
+           emb, leads, head, spr, sel, buf, meta, stage, mem, info, val, acc, flags, xbuf, near, ret, rz, pk, rp, on_s, oc_s,
+           esem, zss, zrs, mss, mrs, iss, irs, xss, xrs, rss, rrs, pss, prs):
     rows, feat = emb.shape
-    half = feat // HALVES
     clusters = hm.shape[1]
     gx = lax.axis_index("group")
     me = lax.axis_index("owner")
@@ -111,7 +111,7 @@
 
     def z_copy(j, f):
         return pltpu.make_async_remote_copy(
-            src_ref=buf.at[j, f], dst_ref=buf.at[NZ + j, f], send_sem=zss.at[j, f], recv_sem=zrs.at[j, f],
+            src_ref=buf.at[j, :, pl.ds(*CUTS[f])], dst_ref=buf.at[NZ + j, :, pl.ds(*CUTS[f])], send_sem=zss.at[j, f], recv_sem=zrs.at[j, f],
             device_id={"owner": z_dev(j)}, device_id_type=MESH)
 
     def m_copy(j):
@@ -121,7 +121,7 @@
 
     def i_copy(j, f, e):
         return pltpu.make_async_remote_copy(
-            src_ref=stage.at[j, f, e], dst_ref=mem.at[0:3, j, e, :, pl.ds(f * half, half)],
+            src_ref=stage.at[j, e, :, :, pl.ds(*CUTS[f])], dst_ref=mem.at[0:3, j, e, :, pl.ds(*CUTS[f])],
             send_sem=iss.at[j, f, e], recv_sem=irs.at[j, f, e],
             device_id={"owner": w_dev(e, 1)}, device_id_type=MESH)
 
@@ -130,8 +130,7 @@
         pick = hot(iota((cap, rows), 0) + j * cap == info[3:4, :].astype(I32))
         x = dot(pick, emb[...])
         x = x * lax.rsqrt(jnp.mean(x * x, axis=-1, keepdims=True) + EPS)
-        for f in range(HALVES):
-            buf[j, f] = x[:, f * half:(f + 1) * half].astype(BF16)
+        buf[j] = x.astype(BF16)
         notes = dot_t(val[...], pick)[0:8]
         meta[j, :, 0:cap] = jnp.where(iota((8, cap), 0) == 2, over, notes)
 
@@ -174,6 +173,7 @@
             block = mem[k, j].reshape(group, feat)
             lead = dot_t(first, block[:, 0:128])
             flags[...] = jnp.maximum(flags[...], lead)
+            leads[k] = jnp.where((lead < 64.0) & used, 0.0, NEG)[0:1]
             acc[k] += dot(hot((lead < 64.0) & used), block)
 
     def spread(j, slot):
@@ -186,15 +186,17 @@
         spr[...] = wide.astype(BF16)
 
     def piece(j, slot, f):
-        out = dot(spr[...], buf[slot, f])
+        lo, wide = CUTS[f]
+        out = dot(spr[...], buf[slot, :, lo:lo + wide])
         if f == 0:
-            stage[j, f, :, :, :, 0:128] = (out[:, 0:128] + head[...]).astype(BF16).reshape(NW, 3, RANKS, 128)
-            stage[j, f, :, :, :, 128:] = out[:, 128:].astype(BF16).reshape(NW, 3, RANKS, half - 128)
+            first_lanes = (out[:, 0:128] + head[...]).astype(BF16)
+            stage[j, :, :, :, 0:128] = first_lanes.reshape(NW, 3, RANKS, 128)
+            stage[j, :, :, :, 128:wide] = out[:, 128:].astype(BF16).reshape(NW, 3, RANKS, wide - 128)
         else:
-            stage[j, f] = out.astype(BF16).reshape(NW, 3, RANKS, half)
-        for e in range(1, NW):
+            stage[j, :, :, :, lo:lo + wide] = out.astype(BF16).reshape(NW, 3, RANKS, wide)
+        for e in (4, 5, 2, 6, 3, 7, 1):
             i_copy(j, f, e).start()
-        mem[0:3, j, 0, :, f * half:(f + 1) * half] = stage[j, f, 0]
+        mem[0:3, j, 0, :, lo:lo + wide] = stage[j, 0, :, :, lo:lo + wide]
 
     def step(j, _):
         @pl.when(j > 0)
@@ -258,11 +260,15 @@
     def score_last(k, _):
         every = mem[k].reshape(n, feat)
         last = every[early:]
-        s = dot_t(every, last) + gone(every)
-        s = jnp.where(iota((n, group), 0) == early + iota((n, group), 1), NEG, s)
+        both = dot_t(every, last)
+        s = jnp.where(iota((n, group), 0) == early + iota((n, group), 1), NEG, both + gone(every))
         near[k, :, early:n] = jnp.max(s, axis=0, keepdims=True)
-        s = dot_t(last, every[0:early]) + gone(last)
-        near[k, :, 0:early] = jnp.maximum(near[k, :, 0:early], jnp.max(s, axis=0, keepdims=True))
+        best = jnp.max(both[0:early] + leads[k], axis=1, keepdims=True)
+        diagonal = iota((group, group), 0) == iota((group, group), 1)
+        for i in range(NZ - 1):
+            part = jnp.where(diagonal, best[i * group:(i + 1) * group], NEG)
+            lanes = pl.ds(i * group, group)
+            near[k, :, lanes] = jnp.maximum(near[k, :, lanes], jnp.max(part, axis=0, keepdims=True))
         return 0
 
     lax.fori_loop(0, 4, score_last, 0)
@@ -271,9 +277,7 @@
         x_copy(k, lax.rem(gx - k + NX, NX)).wait_recv()
     totals = ((xbuf[0] + xbuf[1]) + xbuf[2]) + xbuf[3]
     centroids = totals * lax.rsqrt(jnp.mean(totals * totals, axis=-1, keepdims=True) + EPS)
-    cent_v[...] = centroids[0:4]
-    cent_out = pltpu.make_async_copy(cent_v, cent_o, osem.at[0])
-    cent_out.start()
+    cent_o[...] = centroids[0:4]
     flag_o[0, 0] = jnp.max(totals[4:5, 0:128]).astype(I32)
     lowc = jnp.concatenate([centroids, centroids], axis=0).astype(BF16)
     for k in range(4):
@@ -319,14 +323,11 @@
     both = jnp.concatenate([high, (back - high.astype(F32)).astype(BF16)], axis=0)
     lane = (info[0:1, :].astype(I32) >> 5) * RANKS + info[1:2, :].astype(I32)
     mine = iota((128, rows), 0) == lane
-    outs = [cent_out]
-    for table, out_v, out_ref in ((on_s, near_v, near_o), (oc_s, central_v, central_o)):
+    for table, out_ref in ((on_s, near_o), (oc_s, central_o)):
         took = dot(both, table[...])
         took = jnp.sum(jnp.where(mine, took[0:128] + took[128:256], 0.0), axis=0, keepdims=True)
         for k in range(rows // 128):
-            out_v[k:k + 1, :] = took[:, k * 128:(k + 1) * 128]
-        outs.append(pltpu.make_async_copy(out_v, out_ref, osem.at[len(outs)]))
-        outs[-1].start()
+            out_ref[k:k + 1, :] = took[:, k * 128:(k + 1) * 128]
 
     for j in range(1, NZ):
         m_copy(j).wait_send()
@@ -345,8 +346,6 @@
         return 0
 
     lax.fori_loop(0, NZ, drain, 0)
-    for out in outs:
-        out.wait()
 
 
 def window(cap, collective_id, embeddings, ids, home_map):
@@ -363,18 +362,16 @@
             jax.ShapeDtypeStruct((1, 1), I32),
         ),
         in_specs=[pl.BlockSpec(memory_space=pl.ANY), vmem, vmem],
-        out_specs=(pl.BlockSpec(memory_space=pltpu.HBM),) * 3 + (pl.BlockSpec(memory_space=pltpu.SMEM),),
+        out_specs=(vmem,) * 3 + (pl.BlockSpec(memory_space=pltpu.SMEM),),
         scratch_shapes=[
             pltpu.VMEM((rows, feat), BF16),
-            pltpu.VMEM((4, feat), F32),
-            pltpu.VMEM((rows // 128, 128), F32),
-            pltpu.VMEM((rows // 128, 128), F32),
+            pltpu.VMEM((4, 1, NW * RANKS), F32),
             pltpu.VMEM((NW * 48, 128), F32),
             pltpu.VMEM((NW * 48, cap), BF16),
             pltpu.VMEM((NW * RANKS, 3 * NW * RANKS), BF16),
-            pltpu.VMEM((2 * NZ, HALVES, cap, feat // HALVES), BF16),
+            pltpu.VMEM((2 * NZ, cap, feat), BF16),
             pltpu.VMEM((2 * NZ, 8, lanes), F32),
-            pltpu.VMEM((NZ, HALVES, NW, 3, RANKS, feat // HALVES), BF16),
+            pltpu.VMEM((NZ, NW, 3, RANKS, feat), BF16),
             pltpu.VMEM((4, NZ, NW, RANKS, feat), BF16),
             pltpu.VMEM((8, rows), F32),
             pltpu.VMEM((16, rows), BF16),
@@ -388,7 +385,7 @@
             pltpu.VMEM((2 * NW, 8, 128), F32),
             pltpu.VMEM((128, rows), BF16),
             pltpu.VMEM((128, rows), BF16),
-            dma, dma((3,)), dma((NZ, HALVES)), dma((NZ, HALVES)), dma((NZ,)), dma((NZ,)),
+            dma, dma((NZ, HALVES)), dma((NZ, HALVES)), dma((NZ,)), dma((NZ,)),
             dma((NZ, HALVES, NW)), dma((NZ, HALVES, NW)),
             dma((NX,)), dma((NX,)), dma((NZ,)), dma((NZ,)), dma((NW,)), dma((NW,)),
         ],

time: 143 us -> 143 us (level)
  no operation moved by 1% of the time
where the time goes in v4:
time: 143 us
  Pallas kernels  139 us (97%)
  local copies, waits for them, and re-layouts  1.81 us (1%)
    pallas_call x1, Pallas kernels, window(): pl.pallas_call(functools.partial(kernel, cap), out_shape=(jax.ShapeDtypeS...  139 us

profile of v4, /device:TPU:1, one launch (start us, length us, event | category | flops | bytes accessed | tf_op | source)
XLA Modules:
  0.0 142.7 jit_solution(2489750089920421324)
XLA Ops:
  0.6 0.0 copy-start.1
  0.6 0.0 copy-start
  0.7 139.3 %shard_map.58 = (f32[4,1024]{1,0:T(4,128)S(1)}, f32[12,128]{1,0:T(8,128)S(1)}, f32[12,128]{1,0:T(8,128)S(1)}, s32[1,1]{1,0:T(1,128)}) custom-call(bf16[1536,1024]{1,0:T(8,128)(2,1)} %emb_hbm.1, s32[1,1536]{1,0:T(1,128)} %bitcast.5, s32[1,256]{1,0:T(1,128)} %bitcast.9), custom_call_target="tpu_custom_call" | custom-call | tf_op jit(solution)/shard_map/pallas_call | solution.py:356
  140.7 0.0 copy-done.1
  140.7 0.0 copy-done
  140.7 0.2 conditional.1
  140.9 0.6 copy.15
  141.5 0.6 copy.16
  142.1 0.6 copy.17
Async XLA Ops:
  0.6 140.1 %copy-start.1 = (s32[256]{0:T(256)S(1)}, s32[256]{0:T(256)}, u32[]{:S(2)}) copy-start(s32[256]{0:T(256)} %param.7) | copy-start | bytes 3076
  0.6 140.1 %copy-start = (s32[1536,1]{0,1:T(1,128)S(1)}, s32[1536,1]{0,1:T(1,128)}, u32[]{:S(2)}) copy-start(s32[1536,1]{0,1:T(1,128)} %param.6) | copy-start | bytes 18436
